TPU v7x, 768 devices: a whole 4x8x12 slice. The times are simulated.
768 devices in a mesh: ctx: 32 (over y, x), exp: 12 (over z), tp: 2 (over core).
Axes of the slice: x: 4, y: 8, z: 12, core: 2. Of those that a mesh axis runs over, the one named last changes fastest.
Arguments:
- hidden: bfloat16 [49152, 4, 1408], P(('ctx', 'exp'), None, 'tp'), may hold values from -6 to 6
- expert_ids: int32 [49152, 4], P(('ctx', 'exp')), may hold values from 0 to 63, all different within a row; in each aligned block of 128 rows (0 to 127, 128 to 255, ...) at most 9 rows name the same one
- gate_fix: int32 [49152, 4], P(('ctx', 'exp')), may hold values from 1024 to 65535
- grad_out: bfloat16 [49152, 2048], P(('ctx', 'exp'), 'tp'), may hold values from -6 to 6
- w_down: bfloat16 [64, 1408, 2048], P('ctx', 'tp'), may hold values from -0.15625 to 0.15625
Outputs:
- mixed: bfloat16 [49152, 2048], P(('ctx', 'exp'), 'tp')
- grad_hidden: bfloat16 [49152, 4, 1408], P(('ctx', 'exp'), None, 'tp')
Inputs may be any that keep to these rules, and one draw needn't show every extreme that they name: `expert_ids`: each row names 4 different experts. Within the 128 rows of one index of ctx and exp, no expert is named by more than 9 rows, a bound that some block reaches.
All inputs are finite; a program needn't handle non-finite values.
Results may differ from a plain program's by a relative error of at most 0.013.
Values may be sent and summed in bfloat16 or wider, within the bound.
A program may use at most 64 MiB of HBM per device.

v0:
```python
import jax
import jax.numpy as jnp
from jax import lax
from jax.sharding import PartitionSpec as P


def slot_sources(expert_ids, experts, capacity):
    token_rows, top_count = expert_ids.shape
    assigned = token_rows * top_count
    flat_ids = expert_ids.reshape(assigned)
    onehot = (flat_ids[:, None] == jnp.arange(experts, dtype=jnp.int32)[None, :]).astype(jnp.int32)
    before = jnp.cumsum(onehot, axis=0) - onehot
    position = jnp.sum(before * onehot, axis=1)
    target = flat_ids * capacity + position
    empty = jnp.full((experts * capacity,), assigned, jnp.int32)
    sources = empty.at[target].set(jnp.arange(assigned, dtype=jnp.int32))
    return (target, sources)


def body(hidden, expert_ids, gate_fix, grad_out, w_down):
    token_rows, top_count, ff_part = hidden.shape
    d_part = grad_out.shape[1]
    local_experts = w_down.shape[0]
    cycle_size = lax.axis_size("ctx")
    experts = cycle_size * local_experts
    assigned = token_rows * top_count
    capacity = min(token_rows, assigned // experts + max(1, assigned // (8 * experts)))
    width_slots = local_experts * capacity
    target, sources = slot_sources(expert_ids, experts, capacity)
    gate_val = gate_fix.astype(jnp.float32) * (1.0 / 65536.0)
    scaled = (gate_val[:, :, None] * grad_out[:, None, :].astype(jnp.float32)).astype(jnp.bfloat16)
    scaled = scaled.reshape(assigned, d_part)
    hid_send = jnp.take(
        hidden.reshape(assigned, ff_part), sources, axis=0, mode="fill", fill_value=0
    )
    dy_send = jnp.take(scaled, sources, axis=0, mode="fill", fill_value=0)
    hid_send = hid_send.reshape(cycle_size, width_slots, ff_part)
    dy_send = dy_send.reshape(cycle_size, width_slots, d_part)
    hid_recv, dy_recv = (
        lax.all_to_all(hid_send, "ctx", split_axis=0, concat_axis=0, tiled=True),
        lax.all_to_all(dy_send, "ctx", split_axis=0, concat_axis=0, tiled=True),
    )
    dy_full = lax.all_gather(dy_recv, "tp", axis=2, tiled=True)
    full_width = dy_full.shape[2]
    hid_four = hid_recv.reshape(cycle_size, local_experts, capacity, ff_part)
    dy_four = dy_full.reshape(cycle_size, local_experts, capacity, full_width)
    part_out = jnp.einsum("slch,lhd->slcd", hid_four, w_down, preferred_element_type=jnp.float32)
    part_out = part_out.reshape(cycle_size, width_slots, full_width)
    out_sum = lax.psum_scatter(part_out.astype(jnp.bfloat16), "tp", scatter_dimension=2, tiled=True)
    grad_part = jnp.einsum("slcd,lhd->slch", dy_four, w_down, preferred_element_type=jnp.float32)
    grad_part = grad_part.astype(jnp.bfloat16).reshape(cycle_size, width_slots, ff_part)
    out_back, grad_back = (
        lax.all_to_all(out_sum, "ctx", split_axis=0, concat_axis=0, tiled=True),
        lax.all_to_all(grad_part, "ctx", split_axis=0, concat_axis=0, tiled=True),
    )
    out_flat = out_back.reshape(experts * capacity, d_part)
    grad_flat = grad_back.reshape(experts * capacity, ff_part)
    out_assign = (
        jnp.take(out_flat, target, axis=0)
        .astype(jnp.float32)
        .reshape(token_rows, top_count, d_part)
    )
    mixed = jnp.sum(gate_val[:, :, None] * out_assign, axis=1).astype(jnp.bfloat16)
    grad_hidden = jnp.take(grad_flat, target, axis=0).reshape(token_rows, top_count, ff_part)
    return (mixed, grad_hidden)


def solution(mesh):
    placed = (
        P(("ctx", "exp"), None, "tp"),
        P(("ctx", "exp"), None),
        P(("ctx", "exp"), None),
        P(("ctx", "exp"), "tp"),
        P("ctx", "tp", None),
    )
    return jax.shard_map(
        body,
        mesh=mesh,
        in_specs=placed,
        out_specs=(P(("ctx", "exp"), "tp"), P(("ctx", "exp"), None, "tp")),
        check_vma=False,
    )
```

profile of v0, /device:TPU:208, one launch (start us, length us, event | category | flops | bytes accessed | tf_op | source)
XLA Modules:
  0.0 217.1 jit_solution(3550881770181628647)
XLA Ops:
  9.9 2.4 %scatter_custom_fusion = s32[576]{0:T(1024)S(1)} fusion(s32[512]{0:T(512)S(1)} %bitcast.48, s32[512]{0:T(512)S(1)} %iota.11, s32[]{:T(128)} %constant.64.clone.1), kind=kCustom, calls=%fused_computation.33 | custom fusion | bytes 2308 | tf_op jit(solution)/shard_map/scatter | solution.py:16
  13.5 2.9 %mul.64 = f32[128,4,1024]{2,1,0:T(4,128)} broadcast(bf16[128,1024]{1,0:T(8,128)(2,1)} %param.8), dimensions={0,2} | broadcast | bytes 2359296 | tf_op jit(solution)/shard_map/mul | solution.py:31
  16.3 2.0 mul.65
  18.5 3.4 %gather_fusion.2 = bf16[576,1024]{1,0:T(8,128)(2,1)} fusion(bf16[512,1024]{1,0:T(8,128)(2,1)S(1)} %multiply_convert_fusion, s32[1024]{0:T(1024)S(1)} %pad_clamp_fusion.1), kind=kCustom, calls=%fused_computation.2 | custom fusion | bytes 2361600 | tf_op jit(solution)/shard_map/jit(_take)/gather | solution.py:36
  21.9 1.4 gather.29
  23.3 1.3 broadcast_select_fusion
  24.7 10.2 %all-to-all-start.2 = ((bf16[32,18,1024]{2,1,0:T(8,128)(2,1)}), bf16[32,18,1024]{2,1,0:T(8,128)(2,1)S(1)}, u32[]{:S(2)}, u32[]{:S(2)}) async-start(bf16[32,18,1024]{2,1,0:T(8,128)(2,1)} %broadcast_select_fusion), calls=%async_computation.3 | async-start | bytes 3145728 | tf_op jit(solution)/shard_map/all_to_all | solution.py:41
  36.1 3.3 %gather_fusion = bf16[576,704]{1,0:T(8,128)(2,1)} fusion(bf16[512,704]{1,0:T(8,128)(2,1)S(1)} %reshape.118, s32[1024]{0:T(1024)S(1)} %pad_clamp_fusion.1), kind=kCustom, calls=%fused_computation | custom fusion | bytes 1624320 | tf_op jit(solution)/shard_map/jit(_take)/gather | solution.py:33
  39.4 1.6 gather.25
  41.0 33.0 %all-to-all-done.2 = bf16[32,18,1024]{2,1,0:T(8,128)(2,1)S(1)} async-done(((bf16[32,18,1024]{2,1,0:T(8,128)(2,1)}), bf16[32,18,1024]{2,1,0:T(8,128)(2,1)S(1)}, u32[]{:S(2)}, u32[]{:S(2)}) %all-to-all-start.2) | async-done | bytes 1179680 | tf_op jit(solution)/shard_map/all_to_all | solution.py:41
  74.0 1.2 copy-done
  75.5 35.7 %all_to_all.20 = bf16[32,18,704]{2,1,0:T(8,128)(2,1)S(1)} all-to-all(bf16[32,18,704]{2,1,0:T(8,128)(2,1)S(1)} %broadcast_select_fusion.1), channel_id=1, replica_groups=mesh['ctx'=32,'exp'=12,'tp'=2] {'ctx'}, dimensions={0} | all-to-all | bytes 1622016 | tf_op jit(solution)/shard_map/all_to_all | solution.py:40
  111.4 4.6 %fusion.4 = bf16[2,32,9,2048]{3,1,2,0:T(8,128)(2,1)S(1)} fusion(bf16[32,2,9,704]{3,0,2,1:T(8,128)(2,1)S(1)} %bitcast.45, bf16[2,704,2048]{2,1,0:T(8,128)(2,1)} %param.9), kind=kOutput, calls=%fused_computation.9 | convolution fusion | flops 1662124032 | bytes 8937472 | tf_op jit(solution)/shard_map/slch,lhd->slcd/dot_general | solution.py:47
  116.0 3.0 %copy.22 = bf16[32,18,2048]{2,1,0:T(8,128)(2,1)} copy(bf16[32,18,2048]{2,0,1:T(8,128)(2,1)S(1)} %bitcast.43) | data formatting | bytes 4718592 | tf_op jit(solution)/shard_map/convert_element_type | solution.py:49
  119.1 3.2 %copy.24 = bf16[32,18,2048]{2,0,1:T(8,128)(2,1)S(1)} copy(bf16[32,18,2048]{2,1,0:T(8,128)(2,1)} %all-gather.2.cloned.1.call-done) | data formatting | bytes 4718592 | tf_op jit(solution)/shard_map/all_gather | solution.py:43
  122.3 4.7 %fusion.7 = bf16[2,32,9,704]{3,1,2,0:T(8,128)(2,1)S(1)} fusion(bf16[32,2,9,2048]{3,0,2,1:T(8,128)(2,1)S(1)} %bitcast.44, bf16[2,704,2048]{2,1,0:T(8,128)(2,1)} %param.9), kind=kOutput, calls=%fused_computation.13 | convolution fusion | flops 1661349888 | bytes 8937472 | tf_op jit(solution)/shard_map/slcd,lhd->slch/dot_general | solution.py:50
  127.5 35.0 %all_to_all.21 = bf16[32,18,704]{2,1,0:T(8,128)(2,1)} all-to-all(bf16[32,18,704]{2,1,0:T(8,128)(2,1)S(1)} %copy.25), channel_id=1, replica_groups=mesh['ctx'=32,'exp'=12,'tp'=2] {'ctx'}, dimensions={0} | all-to-all | bytes 1622016 | tf_op jit(solution)/shard_map/all_to_all | solution.py:54
  162.4 5.5 %all-to-all-start.1 = ((bf16[32,18,1024]{2,1,0:T(8,128)(2,1)}), bf16[32,18,1024]{2,1,0:T(8,128)(2,1)S(1)}, u32[]{:S(2)}, u32[]{:S(2)}) async-start(bf16[32,18,1024]{2,1,0:T(8,128)(2,1)} %reduce-scatter.2.cloned.1.call-done), calls=%async_computation.2 | async-start | bytes 3145728 | tf_op jit(solution)/shard_map/all_to_all | solution.py:53
  168.1 1.7 reshape.123
  169.8 2.0 gather_fusion.3
  172.5 1.3 copy.26
  173.8 31.2 %all-to-all-done.1 = bf16[32,18,1024]{2,1,0:T(8,128)(2,1)S(1)} async-done(((bf16[32,18,1024]{2,1,0:T(8,128)(2,1)}), bf16[32,18,1024]{2,1,0:T(8,128)(2,1)S(1)}, u32[]{:S(2)}, u32[]{:S(2)}) %all-to-all-start.1) | async-done | bytes 1179680 | tf_op jit(solution)/shard_map/all_to_all | solution.py:53
  205.4 2.1 gather_fusion.1
  207.9 2.4 %multiply_reduce_fusion = bf16[128,1024]{1,0:T(8,128)(2,1)} fusion(bf16[128,4,1024]{2,1,0:T(4,128)(2,1)S(1)} %gather.27, f32[128,4]{1,0:T(8,128)S(1)} %copy.15, pred[128,4]{1,0:T(8,128)(4,1)S(1)} %compare_and_fusion), kind=kLoop, calls=%fused_computation.11 | loop fusion | flops 1966080 | bytes 1313280 | tf_op jit(solution)/shard_map/reduce_sum | solution.py:63
  (42 shorter events, 7.7 us)
Async XLA Ops:
  24.7 10.2 %copy-start.1 = (bf16[128,4,704]{0,2,1:T(8,128)(2,1)S(1)}, bf16[128,4,704]{0,2,1:T(8,128)(2,1)}, u32[]{:S(2)}) copy-start(bf16[128,4,704]{0,2,1:T(8,128)(2,1)} %param.5) | copy-start | bytes 2162692
  24.7 49.3 %all-to-all-start.2 = ((bf16[32,18,1024]{2,1,0:T(8,128)(2,1)}), bf16[32,18,1024]{2,1,0:T(8,128)(2,1)S(1)}, u32[]{:S(2)}, u32[]{:S(2)}) async-start(bf16[32,18,1024]{2,1,0:T(8,128)(2,1)} %broadcast_select_fusion), calls=%async_computation.3 | async-start | bytes 3145728 | tf_op jit(solution)/shard_map/all_to_all | solution.py:41
  34.9 84.2 %all-gather.2.cloned.1.call-start = ((), (), s32[]{:S(2)}) async-start(), calls=%async_computation.6 | async-start | bytes 4718592 | tf_op jit(solution)/shard_map/all_gather | solution.py:43
  74.0 1.2 copy-start
  75.2 87.2 %reduce-scatter.2.cloned.1.call-start = ((), (), s32[]{:S(2)}) async-start(), calls=%async_computation.5 | async-start | bytes 4718592 | tf_op jit(solution)/shard_map/reduce_scatter | solution.py:49
  162.4 42.5 %all-to-all-start.1 = ((bf16[32,18,1024]{2,1,0:T(8,128)(2,1)}), bf16[32,18,1024]{2,1,0:T(8,128)(2,1)S(1)}, u32[]{:S(2)}, u32[]{:S(2)}) async-start(bf16[32,18,1024]{2,1,0:T(8,128)(2,1)} %reduce-scatter.2.cloned.1.call-done), calls=%async_computation.2 | async-start | bytes 3145728 | tf_op jit(solution)/shard_map/all_to_all | solution.py:53
Sparse Core Ops, SparseCore 0:
  75.4 23.0 all-gather.1
  119.2 21.1 reduce-scatter.1
where the time goes:
time: 218 us; the launch traced here: 217 us
  blocking collectives  70.7 us (32%)
  waiting for transfers between devices  64.3 us (29%)
  local copies, waits for them, and re-layouts  36.1 us (17%)
  starting transfers between devices  15.8 us (7%)
  between operations  14.3 us (7%)
  matrix products  9.31 us (4%)
  other arithmetic  6.65 us (3%)
    all_to_all x1, blocking collectives, body(): lax.all_to_all(hid_send, 'ctx', split_axis=0, concat_axis=0, tiled=True)  35.7 us
    all_to_all x1, blocking collectives, body(): lax.all_to_all(grad_part, 'ctx', split_axis=0, concat_axis=0, tiled=True)  35 us
    all_to_all x1, waiting for transfers between devices, body(): lax.all_to_all(dy_send, 'ctx', split_axis=0, concat_axis=0, tiled=True)  33 us
    all_to_all x1, waiting for transfers between devices, body(): lax.all_to_all(out_sum, 'ctx', split_axis=0, concat_axis=0, tiled=True)  31.2 us
    all_to_all x1, starting transfers between devices, body(): lax.all_to_all(dy_send, 'ctx', split_axis=0, concat_axis=0, tiled=True)  10.2 us
    all_to_all x1, starting transfers between devices, body(): lax.all_to_all(out_sum, 'ctx', split_axis=0, concat_axis=0, tiled=True)  5.5 us
    gather x2, local copies, waits for them, and re-layouts, body(): jnp.take(hidden.reshape(assigned, ff_part), sources, axis=0, mode='fill',...  4.9 us
    gather x2, local copies, waits for them, and re-layouts, body(): dy_send = jnp.take(scaled, sources, axis=0, mode='fill', fill_value=0)  4.84 us
  transfers between devices with their start and end apart: 4, of which 2 were waited for; matrix products, arithmetic and copies ran while one was open for 13% of the time, Pallas kernels for 0%

commit v1 on v0

v1 whole, which is shorter than its diff:
```python
import jax
import jax.numpy as jnp
from jax import lax
from jax.experimental import pallas as pl
from jax.experimental.pallas import tpu as pltpu
from jax.sharding import PartitionSpec as P

MESH = pl.DeviceIdType.MESH
BF16 = jnp.bfloat16
F32 = jnp.float32

NX, NY = 4, 8
CHIPS = NX * NY
EXPERTS = 64
TOK = 128
TOPK = 4
DH = 1024
FH = 704
ROW = 1792
PIECE = 256
NPIECE = ROW // PIECE
COLS = ROW + PIECE
FAR = 12
SELF = 20


def dot(a, b, ca=1, cb=0):
    return lax.dot_general(a, b, (((ca,), (cb,)), ((), ())), preferred_element_type=F32)


def iota(shape, dim):
    return lax.broadcasted_iota(jnp.int32, shape, dim)


def onehot_bf16(mask):
    return jnp.where(mask, 1.0, 0.0).astype(BF16)


def fold(rows, groups, j):
    return onehot_bf16(iota((rows, groups), 0) == iota((rows, groups), 1) * 8 + j)


def unfold(groups, rows, j):
    return onehot_bf16(iota((groups, rows), 1) == iota((groups, rows), 0) * 8 + j)


def slots(ids_ref):
    upper = onehot_bf16(iota((TOK, TOK), 0) < iota((TOK, TOK), 1))
    carry = jnp.zeros((EXPERTS, 1), F32)
    out = []
    for k in range(TOPK):
        ids = ids_ref[k : k + 1, :]
        hot = jnp.where(iota((EXPERTS, TOK), 0) == ids, 1.0, 0.0)
        before = dot(hot.astype(BF16), upper) + carry
        pos = jnp.sum(hot * before, axis=0, keepdims=True).astype(jnp.int32)
        carry = carry + jnp.sum(hot, axis=1, keepdims=True)
        main = jnp.where(pos < 8, ids * 8 + pos, -1)
        last = jnp.where(pos == 8, ids, -1)
        out.append((main, last))
    return out


def pack_kernel(hid_ref, ids_ref, gate_ref, grad_ref, send_ref):
    where = slots(ids_ref)
    rows = EXPERTS * 8
    for last, count in ((False, rows), (True, EXPERTS)):
        hid = jnp.zeros((count, FH), F32)
        pick = jnp.zeros((count, TOK), F32)
        gates = jnp.zeros((count, TOK), F32)
        for k in range(TOPK):
            hit = iota((count, TOK), 0) == where[k][int(last)]
            gate = gate_ref[k : k + 1, :].astype(F32) * (1.0 / 65536.0)
            hot = jnp.where(hit, 1.0, 0.0)
            pick = pick + hot
            gates = gates + jnp.where(hit, gate, 0.0)
            hid = hid + dot(hot.astype(BF16), hid_ref[k], 1, 1)
        gate_col = jnp.sum(gates, axis=1, keepdims=True)
        dy = dot(pick.astype(BF16), grad_ref[...]) * gate_col
        if not last:
            send_ref[:, 0:DH] = dy.astype(BF16)
            send_ref[:, DH:ROW] = jnp.concatenate(
                [hid, jnp.zeros((count, ROW - DH - FH), F32)], axis=1
            ).astype(BF16)
        else:
            whole = jnp.concatenate(
                [dy, hid, jnp.zeros((count, ROW - DH - FH), F32)], axis=1
            ).astype(BF16)
            extra = jnp.zeros((rows, PIECE), F32)
            for j in range(NPIECE):
                extra = extra + dot(fold(rows, EXPERTS, j), whole[:, j * PIECE : (j + 1) * PIECE])
            send_ref[:, ROW:COLS] = extra.astype(BF16)


def combine_kernel(back_ref, ids_ref, gate_ref, mixed_ref, grad_hid_ref):
    where = slots(ids_ref)
    rows = EXPERTS * 8
    extra = back_ref[:, ROW:COLS]
    last_rows = jnp.concatenate(
        [dot(unfold(EXPERTS, rows, j), extra) for j in range(NPIECE)], axis=1
    ).astype(BF16)
    high = [jnp.zeros((n, TOK), F32) for n in (rows, EXPERTS)]
    low = [jnp.zeros((n, TOK), F32) for n in (rows, EXPERTS)]
    main_hid = back_ref[:, DH : DH + FH]
    last_hid = last_rows[:, DH : DH + FH]
    for k in range(TOPK):
        gate = gate_ref[k : k + 1, :]
        top = (gate // 256) * 256
        top_f = top.astype(F32) * (1.0 / 65536.0)
        bot_f = (gate - top).astype(F32) * (1.0 / 65536.0)
        hits = [iota((n, TOK), 0) == where[k][i] for i, n in enumerate((rows, EXPERTS))]
        for i in range(2):
            high[i] = high[i] + jnp.where(hits[i], top_f, 0.0)
            low[i] = low[i] + jnp.where(hits[i], bot_f, 0.0)
        grad_hid_ref[k] = (
            dot(main_hid, onehot_bf16(hits[0]), 0, 0) + dot(last_hid, onehot_bf16(hits[1]), 0, 0)
        ).astype(BF16)
    main_out = back_ref[:, 0:DH]
    last_out = last_rows[:, 0:DH]
    total = dot(high[0].astype(BF16), main_out, 0, 0) + dot(low[0].astype(BF16), main_out, 0, 0)
    total = total + dot(high[1].astype(BF16), last_out, 0, 0) + dot(low[1].astype(BF16), last_out, 0, 0)
    mixed_ref[...] = total.astype(BF16)


def exchange_kernel(
    send_ref, w_ref, back_ref, recv, ret, weights, lhs, last_res,
    w_send, w_recv, own_sem, go_send, go_recv, ret_send, ret_recv,
):
    me = lax.axis_index("ctx")
    core = lax.axis_index("tp")
    y, x = me // NX, lax.rem(me, NX)

    def chip(q, sign):
        dy = lax.rem(q // NX + 3, NY)
        dx = lax.rem(q, NX)
        return lax.rem(y + sign * dy + NY, NY) * NX + lax.rem(x + sign * dx + NX, NX)

    def others(lo, hi, body):
        if lo <= SELF < hi:
            lax.fori_loop(lo, SELF, lambda q, c: body(q), None)
            lax.fori_loop(SELF + 1, hi, lambda q, c: body(q), None)
        else:
            lax.fori_loop(lo, hi, lambda q, c: body(q), None)

    def rows(i):
        return pl.ds(pl.multiple_of(i * 8, 8), 8)

    barrier = pltpu.get_barrier_semaphore()

    def greet(q):
        for e in range(2):
            pl.semaphore_signal(
                barrier, inc=1, device_id={"ctx": chip(q, -1), "tp": e}, device_id_type=MESH
            )

    others(0, CHIPS, greet)
    pl.semaphore_signal(barrier, inc=1, device_id={"tp": 1 - core}, device_id_type=MESH)
    pl.semaphore_wait(barrier, 2 * CHIPS - 1)

    def go(q, e):
        d = chip(q, -1)
        return pltpu.make_async_remote_copy(
            src_ref=send_ref.at[rows(2 * d + e), :],
            dst_ref=recv.at[core, rows(q), :],
            send_sem=go_send.at[e, q],
            recv_sem=go_recv.at[core, q],
            device_id={"ctx": d, "tp": e},
            device_id_type=MESH,
        )

    def come(q, h):
        return pltpu.make_async_remote_copy(
            src_ref=send_ref.at[rows(0), :],
            dst_ref=recv.at[h, rows(q), :],
            send_sem=go_send.at[h, q],
            recv_sem=go_recv.at[h, q],
            device_id={"ctx": chip(q, 1), "tp": h},
            device_id_type=MESH,
        )

    def start_go(q):
        for e in range(2):
            go(q, e).start()

    others(0, FAR, start_go)
    w_copy = pltpu.make_async_remote_copy(
        src_ref=w_ref.at[1 - core],
        dst_ref=weights.at[core],
        send_sem=w_send,
        recv_sem=w_recv,
        device_id={"tp": 1 - core},
        device_id_type=MESH,
    )
    w_copy.start()
    w_own = pltpu.make_async_copy(w_ref.at[core], weights.at[core], own_sem.at[0])
    w_own.start()
    others(FAR, CHIPS, start_go)
    go(SELF, 1 - core).start()
    self_go = pltpu.make_async_copy(
        send_ref.at[rows(2 * me + core), :], recv.at[core, rows(SELF), :], own_sem.at[1]
    )
    self_go.start()

    def put(q, h):
        return pltpu.make_async_remote_copy(
            src_ref=ret.at[h, rows(q), :],
            dst_ref=back_ref.at[rows(2 * me + core), :],
            send_sem=ret_send.at[h, q],
            recv_sem=ret_recv.at[core, q],
            device_id={"ctx": chip(q, 1), "tp": h},
            device_id_type=MESH,
        )

    def got(q, e):
        return pltpu.make_async_remote_copy(
            src_ref=ret.at[e, rows(q), :],
            dst_ref=back_ref.at[rows(2 * chip(q, -1) + e), :],
            send_sem=ret_send.at[e, q],
            recv_sem=ret_recv.at[e, q],
            device_id={"ctx": chip(q, -1), "tp": e},
            device_id_type=MESH,
        )

    def compute(lo, hi):
        n = hi - lo
        main, pad = 8 * n, -(-n // 8) * 8
        total = main + pad
        first = lo * 8
        for h in range(2):
            lhs[h, 0:main, :] = recv[h, first : first + main, 0:ROW]
            extra = recv[h, first : first + main, ROW:COLS]
            for j in range(NPIECE):
                lhs[h, main:total, j * PIECE : (j + 1) * PIECE] = dot(
                    unfold(pad, main, j), extra
                ).astype(BF16)
        for b in range(4):
            h, at = b // 2, (b % 2) * 512
            cols = slice(b * 512, (b + 1) * 512)
            res = dot(lhs[0, 0:total, DH : DH + FH], weights[0, :, cols])
            res = (res + dot(lhs[1, 0:total, DH : DH + FH], weights[1, :, cols])).astype(BF16)
            ret[h, first : first + main, at : at + 512] = res[0:main]
            last_res[h, 0:pad, at : at + 512] = res[main:total]
        for h in range(2):
            res = dot(lhs[0, 0:total, 0:DH], weights[h, :, 0:DH], 1, 1)
            res = res + dot(lhs[1, 0:total, 0:DH], weights[h, :, DH : 2 * DH], 1, 1)
            res = jnp.concatenate([res, jnp.zeros((total, ROW - DH - FH), F32)], axis=1).astype(BF16)
            ret[h, first : first + main, DH:ROW] = res[0:main]
            last_res[h, 0:pad, DH:ROW] = res[main:total]
            extra = jnp.zeros((main, PIECE), F32)
            for j in range(NPIECE):
                extra = extra + dot(
                    fold(main, pad, j), last_res[h, 0:pad, j * PIECE : (j + 1) * PIECE]
                )
            ret[h, first : first + main, ROW:COLS] = extra.astype(BF16)

    def wait_come(q):
        for h in range(2):
            come(q, h).wait_recv()

    def start_put(q):
        for h in range(2):
            put(q, h).start()

    others(0, FAR, wait_come)
    w_own.wait()
    w_copy.wait_recv()
    compute(0, FAR)
    others(0, FAR, start_put)

    others(FAR, CHIPS, wait_come)
    come(SELF, 1 - core).wait_recv()
    self_go.wait()
    compute(FAR, CHIPS)
    others(FAR, CHIPS, start_put)
    put(SELF, 1 - core).start()
    self_put = pltpu.make_async_copy(
        ret.at[core, rows(SELF), :], back_ref.at[rows(2 * me + core), :], own_sem.at[2]
    )
    self_put.start()

    def drain(q):
        for e in range(2):
            go(q, e).wait_send()
            put(q, e).wait_send()
            got(q, e).wait_recv()

    others(0, CHIPS, drain)
    go(SELF, 1 - core).wait_send()
    put(SELF, 1 - core).wait_send()
    got(SELF, 1 - core).wait_recv()
    self_put.wait()
    w_copy.wait_send()


def vmem(n):
    return [pl.BlockSpec(memory_space=pltpu.VMEM)] * n


def body(hidden, expert_ids, gate_fix, grad_out, w_down):
    hid_t = jnp.transpose(hidden, (1, 2, 0))
    ids_t = jnp.transpose(expert_ids)
    gate_t = jnp.transpose(gate_fix)
    rows = EXPERTS * 8
    send = pl.pallas_call(
        pack_kernel,
        out_shape=jax.ShapeDtypeStruct((rows, COLS), BF16),
        in_specs=vmem(4),
        out_specs=vmem(1)[0],
        name="pack",
    )(hid_t, ids_t, gate_t, grad_out)
    back = pl.pallas_call(
        exchange_kernel,
        out_shape=jax.ShapeDtypeStruct((rows, COLS), BF16),
        in_specs=[vmem(1)[0], pl.BlockSpec(memory_space=pl.ANY)],
        out_specs=pl.BlockSpec(memory_space=pl.ANY),
        scratch_shapes=[
            pltpu.VMEM((2, CHIPS * 8, COLS), BF16),
            pltpu.VMEM((2, CHIPS * 8, COLS), BF16),
            pltpu.VMEM((2, FH, 2 * DH), BF16),
            pltpu.VMEM((2, 184, ROW), BF16),
            pltpu.VMEM((2, 24, ROW), BF16),
            pltpu.SemaphoreType.DMA,
            pltpu.SemaphoreType.DMA,
            pltpu.SemaphoreType.DMA((3,)),
            pltpu.SemaphoreType.DMA((2, CHIPS)),
            pltpu.SemaphoreType.DMA((2, CHIPS)),
            pltpu.SemaphoreType.DMA((2, CHIPS)),
            pltpu.SemaphoreType.DMA((2, CHIPS)),
        ],
        compiler_params=pltpu.CompilerParams(collective_id=0, has_side_effects=True),
        name="exchange",
    )(send, w_down)
    mixed, grad_t = pl.pallas_call(
        combine_kernel,
        out_shape=(
            jax.ShapeDtypeStruct((TOK, DH), BF16),
            jax.ShapeDtypeStruct((TOPK, FH, TOK), BF16),
        ),
        in_specs=vmem(3),
        out_specs=tuple(vmem(2)),
        name="combine",
    )(back, ids_t, gate_t)
    return mixed, jnp.transpose(grad_t, (2, 0, 1))


def solution(mesh):
    placed = (
        P(("ctx", "exp"), None, "tp"),
        P(("ctx", "exp"), None),
        P(("ctx", "exp"), None),
        P(("ctx", "exp"), "tp"),
        P("ctx", "tp", None),
    )
    return jax.shard_map(
        body,
        mesh=mesh,
        in_specs=placed,
        out_specs=(P(("ctx", "exp"), "tp"), P(("ctx", "exp"), None, "tp")),
        check_vma=False,
    )
```

time: 218 us -> 124 us (0.57)
  the two profiles are of different devices: /device:TPU:208 before, /device:TPU:1 now
where the time goes in v1:
time: 124 us; the launch traced here: 123 us
  Pallas kernels  123 us (99%)
    pallas_call x1, Pallas kernels, body(): pl.pallas_call(exchange_kernel, out_shape=jax.ShapeDtypeStruct((rows, COL...  113 us
    pallas_call x1, Pallas kernels, body(): pl.pallas_call(pack_kernel, out_shape=jax.ShapeDtypeStruct((rows, COLS),...  5.31 us
    pallas_call x1, Pallas kernels, body(): pl.pallas_call(combine_kernel, out_shape=(jax.ShapeDtypeStruct((TOK, DH),...  4.56 us

profile of v1, /device:TPU:1, one launch (start us, length us, event | category | flops | bytes accessed | tf_op | source)
XLA Modules:
  0.0 123.3 jit_solution(17857373459445386832)
XLA Ops:
  0.6 5.3 %pack.1.send_ref = bf16[512,2048]{1,0:T(8,128)(2,1)} custom-call(bf16[4,704,128]{2,1,0:T(8,128)(2,1)} %bitcast.4, s32[4,128]{1,0:T(4,128)} %bitcast.5, s32[4,128]{1,0:T(4,128)} %bitcast.7, bf16[128,1024]{1,0:T(8,128)(2,1)} %grad_ref.1), custom_call_target="tpu_custom_call" | custom-call | tf_op jit(solution)/shard_map/pack/pallas_call | solution.py:303
  5.9 112.8 %exchange.1.back_ref = bf16[512,2048]{1,0:T(8,128)(2,1)} custom-call(bf16[512,2048]{1,0:T(8,128)(2,1)} %pack.1.send_ref, bf16[2,704,2048]{2,1,0:T(8,128)(2,1)} %w_ref.1), custom_call_target="tpu_custom_call" | custom-call | tf_op jit(solution)/shard_map/exchange/pallas_call | solution.py:310
  118.7 4.6 %combine.1 = (bf16[128,1024]{1,0:T(8,128)(2,1)}, bf16[4,704,128]{2,1,0:T(8,128)(2,1)}) custom-call(bf16[512,2048]{1,0:T(8,128)(2,1)} %exchange.1.back_ref, s32[4,128]{1,0:T(4,128)} %bitcast.6, s32[4,128]{1,0:T(4,128)} %bitcast.8), custom_call_target="tpu_custom_call" | custom-call | tf_op jit(solution)/shard_map/combine/pallas_call | solution.py:332
